TPU v7x, 32 devices: a whole 2x2x4 slice. The times are simulated.
32 devices in a mesh: shot: 16 (over z, x, core), freq: 2 (over y).
Axes of the slice: x: 2, y: 2, z: 4, core: 2. Of those that a mesh axis runs over, the one named last changes fastest.
Arguments:
- wavefield: bfloat16 [4, 6144, 1024], P('freq', 'shot'), parts along dimension 0, may hold values from -0.8984375 to 0.8984375
- recorded: bfloat16 [6, 2, 2, 6144, 384], P('freq', None, None, 'shot'), parts along dimension 0, may hold values from -6 to 6
- match_filter: bfloat16 [2, 63], replicated, may hold values from -0.5 to 0.5
Outputs:
- demultiple: bfloat16 [6, 2, 2, 6144, 384], P('freq', None, None, 'shot'), parts along dimension 0
There are 2 independent parts, one for each index of `freq`. A program takes and returns all parts, laid end to end along the dimension named above; an argument that names none is the same for every part. Nothing has to cross between parts.
All inputs are finite; a program needn't handle non-finite values.
Results may differ from a plain program's by a relative error of at most 0.0048.
Values may be sent and summed in bfloat16 or wider, within the bound.
A program may use at most 64 MiB of HBM per device.

v0:
```python
import jax
import jax.numpy as jnp
from jax import lax
from jax.sharding import PartitionSpec as P


def passed_along(value, axis, steps):
    count = lax.axis_size(axis)
    pairs = [(source, (source + steps) % count) for source in range(count)]
    return lax.ppermute(value, axis, pairs)


def toeplitz(match_filter, block_span_width):
    tap_count = match_filter.shape[1]
    half_taps = (tap_count - 1) // 2
    row_index = lax.broadcasted_iota(jnp.int32, (block_span_width, block_span_width), 0)
    col_index = lax.broadcasted_iota(jnp.int32, (block_span_width, block_span_width), 1)
    lag_index = row_index - col_index + half_taps
    coeffs = match_filter.astype(jnp.float32)

    def place_tap(tap_index, carried):
        column = lax.dynamic_slice_in_dim(coeffs, tap_index, 1, 1)
        return jnp.where((lag_index == tap_index)[None], column[:, :, None], carried)

    return lax.fori_loop(
        0, tap_count, place_tap, jnp.zeros((2, block_span_width, block_span_width), jnp.float32)
    )


def filter_weights(match_filter, block_span_width):
    toe_pair = toeplitz(match_filter, block_span_width)
    real_component = toe_pair[0].astype(jnp.bfloat16)
    imag_part = toe_pair[1].astype(jnp.bfloat16)
    return jnp.stack(
        [jnp.stack([real_component, imag_part], 1), jnp.stack([-imag_part, real_component], 1)], 0
    )


def shards(wavefield, recorded, match_filter):
    cycle_size = lax.axis_size("shot")
    block_span_width = wavefield.shape[1]
    weights = filter_weights(match_filter, block_span_width)
    real_component = wavefield[0]
    imag_part = wavefield[1]
    left_rows = jnp.concatenate(
        [
            jnp.concatenate([real_component, -imag_part], 1),
            jnp.concatenate([imag_part, real_component], 1),
        ],
        0,
    )
    results = []
    for slot_index, offset in enumerate((1, cycle_size // 8, cycle_size // 4)):
        ahead_data = passed_along(wavefield, "shot", -offset)
        right_rows = jnp.concatenate([ahead_data[0], ahead_data[1]], 1)
        stacked = lax.dot_general(
            left_rows, right_rows, (((1,), (1,)), ((), ())), preferred_element_type=jnp.float32
        )
        forward_tile = stacked.astype(jnp.bfloat16).reshape(2, block_span_width, block_span_width)
        ahead_filtered = jnp.einsum(
            "csq,cqdx->dsx", forward_tile, weights, preferred_element_type=jnp.float32
        )
        received = passed_along(forward_tile, "shot", offset)
        behind_filtered = jnp.einsum(
            "csr,csdx->drx", received, weights, preferred_element_type=jnp.float32
        )
        ahead_out = (recorded[slot_index, 0].astype(jnp.float32) - ahead_filtered).astype(
            jnp.bfloat16
        )
        behind_out = (recorded[slot_index, 1].astype(jnp.float32) - behind_filtered).astype(
            jnp.bfloat16
        )
        results.append(jnp.stack([ahead_out, behind_out]))
    return jnp.stack(results)


def solution(mesh):
    return jax.shard_map(
        shards,
        mesh=mesh,
        in_specs=(P("freq", "shot", None), P("freq", None, None, "shot", None), P()),
        out_specs=P("freq", None, None, "shot", None),
        check_vma=False,
    )
```

profile of v0, /device:TPU:0, one launch (start us, length us, event | category | flops | bytes accessed | tf_op | source)
XLA Modules:
  0.0 121.3 jit_solution(17144111786377696996)
XLA Ops:
  0.0 5.4 %collective-permute-start = (bf16[2,384,1024]{2,1,0:T(8,128)(2,1)}, bf16[2,384,1024]{2,1,0:T(8,128)(2,1)}, u32[]{:S(2)}, u32[]{:S(2)}) collective-permute-start(bf16[2,384,1024]{2,1,0:T(8,128)(2,1)} %param.5), channel_id=1, source_target_pairs={{0,30},{2,0},{4,2},{6,4},{8,6},{10,8},{12,10},{14,12},{16,14},{18,... | collective-permute-start | bytes 4718600 | tf_op jit(solution)/shard_map/ppermute | solution.py:10
  5.4 0.4 collective-permute-start.4
  5.9 0.6 collective-permute-start.2
  6.5 0.8 copy.5
  7.2 34.9 %while.14 = (s32[]{:T(128)}, bf16[2,384,384]{2,1,0:T(8,128)(2,1)S(1)}, bf16[2,63]{0,1:T(8,128)(2,1)S(1)}, s32[]{:T(128)}, s32[]{:T(128)}) while((s32[]{:T(128)}, bf16[2,384,384]{2,1,0:T(8,128)(2,1)S(1)}, bf16[2,63]{0,1:T(8,128)(2,1)S(1)}, s32[]{:T(128)}, s32[]{:T(128)}) %tuple.43), condition=%wide.region_1.2_spmd.clone, body=%wide.region_0.1_spmd.clone.sunk | while | flops 1032195 | bytes 1474659 | solution.py:25
  14.0 0.4 select_select_fusion.2
  42.5 3.2 %fusion.49 = (bf16[1,1,2,384,384]{4,3,2,1,0:T(8,128)(2,1)}, bf16[1,1,2,384,384]{4,3,2,1,0:T(8,128)(2,1)S(1)}, bf16[1,1,2,384,384]{4,3,2,1,0:T(8,128)(2,1)S(1)}, ...) fusion(bf16[3,2,2,384,384]{4,3,2,1,0:T(8,128)(2,1)} %param.6), kind=kLoop, calls=%fused_computation.69 | loop fusion | bytes 7077888 | tf_op jit(solution)/shard_map/slice | solution.py:67
  45.7 2.1 %copy.20 = bf16[1,1,2,384,384]{3,4,2,1,0:T(8,128)(2,1)} copy(bf16[1,1,2,384,384]{4,3,2,1,0:T(8,128)(2,1)} %get-tuple-element.105) | data formatting | bytes 1179648
  47.8 1.1 copy.24
  48.9 1.1 copy.23
  50.0 1.1 copy.22
  51.0 1.1 copy.21
  52.5 1.0 copy-done
  53.9 1.5 %slice_bitcast_fusion.5 = (bf16[384,1024]{1,0:T(8,128)(2,1)S(1)}, bf16[384,1024]{1,0:T(8,128)(2,1)S(1)}) fusion(bf16[2,384,1024]{2,1,0:T(8,128)(2,1)} %collective-permute-done), kind=kLoop, calls=%fused_computation.54 | loop fusion | bytes 3145728 | tf_op jit(solution)/shard_map/squeeze | solution.py:55
  55.4 1.8 %fusion.32 = bf16[768,384]{1,0:T(8,128)(2,1)S(1)} fusion(bf16[384,1024]{1,0:T(8,128)(2,1)S(1)} %get-tuple-element.112, bf16[384,1024]{1,0:T(8,128)(2,1)S(1)} %get-tuple-element.111, bf16[384,1024]{1,0:T(8,128)(2,1)S(1)} %get-tuple-element.116, bf16[384,1024]{1,0:T(8,128)(2,1)S(1)} %get-tuple-element.115, bf16[384,1024]{1,0:T(8,128)(2,1)S(1)} %fusion.48), kind=kOutput, calls=%fused_computation.38 | convolution fusion | flops 1223983104 | bytes 4521984 | tf_op jit(solution)/shard_map/dot_general | solution.py:56
  57.2 17.1 %collective-permute-done.4 = bf16[2,384,1024]{2,1,0:T(8,128)(2,1)} collective-permute-done((bf16[2,384,1024]{2,1,0:T(8,128)(2,1)}, bf16[2,384,1024]{2,1,0:T(8,128)(2,1)}, u32[]{:S(2)}, u32[]{:S(2)}) %collective-permute-start.4) | collective-permute-done | bytes 1572896 | tf_op jit(solution)/shard_map/ppermute | solution.py:10
  74.3 1.5 %slice_bitcast_fusion.1 = (bf16[384,1024]{1,0:T(8,128)(2,1)S(1)}, bf16[384,1024]{1,0:T(8,128)(2,1)S(1)}) fusion(bf16[2,384,1024]{2,1,0:T(8,128)(2,1)} %collective-permute-done.4), kind=kLoop, calls=%fused_computation.50 | loop fusion | bytes 3145728 | tf_op jit(solution)/shard_map/squeeze | solution.py:55
  75.8 1.8 %fusion.26 = bf16[768,384]{1,0:T(8,128)(2,1)S(1)} fusion(bf16[384,1024]{1,0:T(8,128)(2,1)S(1)} %get-tuple-element.118, bf16[384,1024]{1,0:T(8,128)(2,1)S(1)} %get-tuple-element.117, bf16[384,1024]{1,0:T(8,128)(2,1)S(1)} %get-tuple-element.116, bf16[384,1024]{1,0:T(8,128)(2,1)S(1)} %get-tuple-element.115, bf16[384,1024]{1,0:T(8,128)(2,1)S(1)} %fusion.48), kind=kOutput, calls=%fused_computation.36 | convolution fusion | flops 1223983104 | bytes 4521984 | tf_op jit(solution)/shard_map/dot_general | solution.py:56
  77.7 19.0 %collective-permute-done.2 = bf16[2,384,1024]{2,1,0:T(8,128)(2,1)} collective-permute-done((bf16[2,384,1024]{2,1,0:T(8,128)(2,1)}, bf16[2,384,1024]{2,1,0:T(8,128)(2,1)}, u32[]{:S(2)}, u32[]{:S(2)}) %collective-permute-start.2) | collective-permute-done | bytes 1572896 | tf_op jit(solution)/shard_map/ppermute | solution.py:10
  96.7 1.5 %slice_bitcast_fusion.3 = (bf16[384,1024]{1,0:T(8,128)(2,1)S(1)}, bf16[384,1024]{1,0:T(8,128)(2,1)S(1)}) fusion(bf16[2,384,1024]{2,1,0:T(8,128)(2,1)} %collective-permute-done.2), kind=kLoop, calls=%fused_computation.52 | loop fusion | bytes 3145728 | tf_op jit(solution)/shard_map/squeeze | solution.py:55
  98.2 1.8 %fusion.29 = bf16[768,384]{1,0:T(8,128)(2,1)S(1)} fusion(bf16[384,1024]{1,0:T(8,128)(2,1)S(1)} %get-tuple-element.114, bf16[384,1024]{1,0:T(8,128)(2,1)S(1)} %get-tuple-element.113, bf16[384,1024]{1,0:T(8,128)(2,1)S(1)} %get-tuple-element.116, bf16[384,1024]{1,0:T(8,128)(2,1)S(1)} %get-tuple-element.115, bf16[384,1024]{1,0:T(8,128)(2,1)S(1)} %fusion.48), kind=kOutput, calls=%fused_computation.37 | convolution fusion | flops 1223983104 | bytes 4521984 | tf_op jit(solution)/shard_map/dot_general | solution.py:56
  100.0 0.4 collective-permute-start.3
  100.4 0.8 fusion.35
  101.5 0.8 fusion.39
  102.6 0.8 fusion.37
  103.4 10.0 %collective-permute-done.3 = bf16[2,384,384]{2,1,0:T(8,128)(2,1)S(1)} collective-permute-done((bf16[2,384,384]{2,1,0:T(8,128)(2,1)S(1)}, bf16[2,384,384]{2,1,0:T(8,128)(2,1)S(1)}, u32[]{:S(2)}, u32[]{:S(2)}) %collective-permute-start.3) | collective-permute-done | bytes 589856 | tf_op jit(solution)/shard_map/ppermute | solution.py:10
  113.4 0.8 fusion.38
  114.3 0.9 copy-done.1
  115.2 0.8 fusion.36
  116.2 0.8 fusion.40
  117.1 0.5 pad_maximum_fusion
  117.6 3.7 %copy.13 = bf16[3,2,2,384,384]{4,3,2,1,0:T(8,128)(2,1)} copy(bf16[3,2,2,384,384]{3,4,2,1,0:T(8,128)(2,1)S(1)} %pad_maximum_fusion) | data formatting | bytes 7077888 | tf_op jit(solution)/shard_map/stack | solution.py:74
  (214 shorter events, 35.0 us)
Async XLA Ops:
  0.0 53.9 %collective-permute-start = (bf16[2,384,1024]{2,1,0:T(8,128)(2,1)}, bf16[2,384,1024]{2,1,0:T(8,128)(2,1)}, u32[]{:S(2)}, u32[]{:S(2)}) collective-permute-start(bf16[2,384,1024]{2,1,0:T(8,128)(2,1)} %param.5), channel_id=1, source_target_pairs={{0,30},{2,0},{4,2},{6,4},{8,6},{10,8},{12,10},{14,12},{16,14},{18,... | collective-permute-start | bytes 4718600 | tf_op jit(solution)/shard_map/ppermute | solution.py:10
  5.4 68.9 %collective-permute-start.4 = (bf16[2,384,1024]{2,1,0:T(8,128)(2,1)}, bf16[2,384,1024]{2,1,0:T(8,128)(2,1)}, u32[]{:S(2)}, u32[]{:S(2)}) collective-permute-start(bf16[2,384,1024]{2,1,0:T(8,128)(2,1)} %param.5), channel_id=1, source_target_pairs={{0,24},{2,26},{4,28},{6,30},{8,0},{10,2},{12,4},{14,6},{16,8},{18,... | collective-permute-start | bytes 4718600 | tf_op jit(solution)/shard_map/ppermute | solution.py:10
  5.9 90.8 %collective-permute-start.2 = (bf16[2,384,1024]{2,1,0:T(8,128)(2,1)}, bf16[2,384,1024]{2,1,0:T(8,128)(2,1)}, u32[]{:S(2)}, u32[]{:S(2)}) collective-permute-start(bf16[2,384,1024]{2,1,0:T(8,128)(2,1)} %param.5), channel_id=1, source_target_pairs={{0,28},{2,30},{4,0},{6,2},{8,4},{10,6},{12,8},{14,10},{16,12},{18,... | collective-permute-start | bytes 4718600 | tf_op jit(solution)/shard_map/ppermute | solution.py:10
  52.1 1.4 %copy-start = (bf16[2,384,1024]{2,1,0:T(8,128)(2,1)S(1)}, bf16[2,384,1024]{2,1,0:T(8,128)(2,1)}, u32[]{:S(2)}) copy-start(bf16[2,384,1024]{2,1,0:T(8,128)(2,1)} %param.5) | copy-start | bytes 4718596
  57.2 57.1 %collective-permute-start.1 = (bf16[2,384,384]{2,1,0:T(8,128)(2,1)S(1)}, bf16[2,384,384]{2,1,0:T(8,128)(2,1)S(1)}, u32[]{:S(2)}, u32[]{:S(2)}) collective-permute-start(bf16[2,384,384]{2,1,0:T(8,128)(2,1)S(1)} %bitcast.157), channel_id=1, source_target_pairs={{0,2},{2,4},{4,6},{6,8},{8,10},{10,12},{12,14},{14,16},{16,18},{18... | collective-permute-start | bytes 1769480 | tf_op jit(solution)/shard_map/ppermute | solution.py:10
  77.6 38.5 %collective-permute-start.5 = (bf16[2,384,384]{2,1,0:T(8,128)(2,1)S(1)}, bf16[2,384,384]{2,1,0:T(8,128)(2,1)S(1)}, u32[]{:S(2)}, u32[]{:S(2)}) collective-permute-start(bf16[2,384,384]{2,1,0:T(8,128)(2,1)S(1)} %bitcast.159), channel_id=1, source_target_pairs={{0,8},{2,10},{4,12},{6,14},{8,16},{10,18},{12,20},{14,22},{16,24},... | collective-permute-start | bytes 1769480 | tf_op jit(solution)/shard_map/ppermute | solution.py:10
  98.2 2.3 %copy-start.3 = (bf16[1,1,2,384,384]{3,4,2,1,0:T(8,128)(2,1)S(1)}, bf16[1,1,2,384,384]{3,4,2,1,0:T(8,128)(2,1)}, u32[]{:S(2)}) copy-start(bf16[1,1,2,384,384]{3,4,2,1,0:T(8,128)(2,1)} %copy.20) | copy-start | bytes 1769476
  100.0 13.4 %collective-permute-start.3 = (bf16[2,384,384]{2,1,0:T(8,128)(2,1)S(1)}, bf16[2,384,384]{2,1,0:T(8,128)(2,1)S(1)}, u32[]{:S(2)}, u32[]{:S(2)}) collective-permute-start(bf16[2,384,384]{2,1,0:T(8,128)(2,1)S(1)} %bitcast.161), channel_id=1, source_target_pairs={{0,4},{2,6},{4,8},{6,10},{8,12},{10,14},{12,16},{14,18},{16,20},{1... | collective-permute-start | bytes 1769480 | tf_op jit(solution)/shard_map/ppermute | solution.py:10
  100.4 1.1 copy-start.4
  101.5 1.1 copy-start.5
  102.6 10.8 %copy-start.2 = (bf16[1,1,2,384,384]{3,4,2,1,0:T(8,128)(2,1)S(1)}, bf16[1,1,2,384,384]{3,4,2,1,0:T(8,128)(2,1)}, u32[]{:S(2)}) copy-start(bf16[1,1,2,384,384]{3,4,2,1,0:T(8,128)(2,1)} %copy.23) | copy-start | bytes 1769476
  114.2 1.1 copy-start.1
where the time goes:
time: 122 us; the launch traced here: 121 us
  waiting for transfers between devices  46.1 us (38%)
  other arithmetic  33.7 us (28%)
  local copies, waits for them, and re-layouts  22.5 us (18%)
  matrix products  10.1 us (8%)
  starting transfers between devices  7.01 us (6%)
  loops' own time  1.65 us (1%)
    ppermute x6, waiting for transfers between devices, passed_along(): return lax.ppermute(value, axis, pairs)  46.1 us
    select_n x63, other arithmetic, place_tap(): jnp.where((lag_index == tap_index)[None], column[:, :, None], carried)  24.5 us
    unnamed x19, local copies, waits for them, and re-layouts  9.93 us
    eq x63, other arithmetic, place_tap(): lag_index == tap_index  8.06 us
    ppermute x6, starting transfers between devices, passed_along(): return lax.ppermute(value, axis, pairs)  7.01 us
    dot_general x3, matrix products, shards(): lax.dot_general(left_rows, right_rows, (((1,), (1,)), ((), ())), preferre...  5.42 us
    squeeze x3, local copies, waits for them, and re-layouts, shards(): right_rows = jnp.concatenate([ahead_data[0], ahead_data[1]], 1)  4.47 us
    another operation x1, local copies, waits for them, and re-layouts, shards(): return jnp.stack(results)  3.68 us
  transfers between devices with their start and end apart: 6, of which 3 were waited for; matrix products, arithmetic and copies ran while one was open for 48% of the time, Pallas kernels for 0%

commit v1 on v0

--- a/solution.py
+++ b/solution.py
@@ -1,7 +1,290 @@
+import functools
+
 import jax
 import jax.numpy as jnp
 from jax import lax
+from jax.experimental import pallas as pl
+from jax.experimental.pallas import tpu as pltpu
 from jax.sharding import PartitionSpec as P
+
+MESH = pl.DeviceIdType.MESH
+STEP = 128
+CH_A, CH_B, CH_C, CH_M, CH_D = range(5)
+F32 = jnp.float32
+BF16 = jnp.bfloat16
+
+
+def dot_t(a, b):
+    return lax.dot_general(a, b, (((1,), (1,)), ((), ())), preferred_element_type=F32)
+
+
+def kernel(
+    n, mf, wave, rec, out,
+    left, weights, buf_a, buf_b, buf_c, buf_m, buf_d,
+    send_a, send_c, recv_a, recv_c, tile, tile2, tile3, rec_v, res,
+    ssem, rsem, in_sem, out_sem,
+):
+    span, depth = wave.shape[1], wave.shape[2]
+    pieces = span // STEP
+    taps = mf.shape[1]
+    half = (taps - 1) // 2
+    me = lax.axis_index("shot")
+    core = lax.rem(me, 2)
+    side = lax.rem(me // 2, 2)
+    mate = me + 1 - 2 * core
+    across = me + 2 - 4 * side
+    up, down = lax.rem(me + 4, n), lax.rem(me + n - 4, n)
+    z_to = (1 - side) * down + side * up
+    z_from = (1 - side) * up + side * down
+    owner = (core == side)
+    giver = (core != side)
+
+    barrier = pltpu.get_barrier_semaphore()
+    for other in (mate, across, up, down):
+        pl.semaphore_signal(barrier, inc=1, device_id={"shot": other}, device_id_type=MESH)
+    pl.semaphore_wait(barrier, 4)
+
+    def remote(src, dst, sem, target):
+        return pltpu.make_async_remote_copy(
+            src_ref=src, dst_ref=dst, send_sem=ssem.at[sem], recv_sem=rsem.at[sem],
+            device_id={"shot": target}, device_id_type=MESH,
+        )
+
+    def rows(i):
+        if isinstance(i, int):
+            return pl.ds(i * STEP, STEP)
+        return pl.ds(pl.multiple_of(i * STEP, STEP), STEP)
+
+    def cols(i, base):
+        return pl.ds(pl.multiple_of(base + i * STEP, STEP), STEP)
+
+    def piece(src, dst, channel, i, target):
+        return remote(
+            src.at[:, rows(i), :], dst.at[:, rows(i), :], channel * pieces + i, target
+        )
+
+    tile_sem = 5 * pieces
+
+    def z_copy(i):
+        return piece(wave, buf_a, CH_A, i, z_to)
+
+    def fwd_copy(i):
+        return piece(buf_a, buf_b, CH_B, i, across)
+
+    def row_copy(i):
+        return piece(wave, buf_c, CH_C, i, across)
+
+    def mate_copy(i):
+        return piece(wave, buf_m, CH_M, i, mate)
+
+    def share_c(i):
+        return piece(buf_c, buf_d, CH_D, i, mate)
+
+    def share_b(i):
+        return piece(buf_b, buf_d, CH_D, i, mate)
+
+    tile_a = remote(send_a, recv_a, tile_sem, z_from)
+    tile_c = remote(send_c, recv_c, tile_sem + 1, across)
+
+    @pl.when(giver)
+    def _():
+        for i in range(pieces):
+            row_copy(i).start()
+
+    for i in range(pieces):
+        z_copy(i).start()
+    for i in range(pieces):
+        mate_copy(i).start()
+    load = pltpu.make_async_copy(rec, rec_v, in_sem)
+    load.start()
+
+    left[:span, :depth] = wave[0]
+    left[:span, depth:] = -wave[1]
+    left[span:, :depth] = wave[1]
+    left[span:, depth:] = wave[0]
+
+    weights[...] = jnp.zeros_like(weights)
+    shape = (STEP, STEP)
+    base_lag = lax.broadcasted_iota(jnp.int32, shape, 0) - lax.broadcasted_iota(jnp.int32, shape, 1)
+    reach = -(-half // STEP) if half else 0
+    for d in range(-reach, reach + 1):
+        if abs(d) >= pieces:
+            continue
+        lag = base_lag + (d * STEP + half)
+
+        def place(tap, carry, lag=lag):
+            hit = lag == tap
+            return (
+                jnp.where(hit, mf[0, tap], carry[0]),
+                jnp.where(hit, mf[1, tap], carry[1]),
+            )
+
+        zero = jnp.zeros(shape, F32)
+        real, imag = lax.fori_loop(0, taps, place, (zero, zero))
+        real, imag = real.astype(BF16), imag.astype(BF16)
+        for bc in range(pieces):
+            br = bc + d
+            if 0 <= br < pieces:
+                r0, c0 = br * STEP, bc * STEP
+                weights[r0:r0 + STEP, c0:c0 + STEP] = real
+                weights[r0:r0 + STEP, span + c0:span + c0 + STEP] = imag
+                weights[span + r0:span + r0 + STEP, c0:c0 + STEP] = -imag
+                weights[span + r0:span + r0 + STEP, span + c0:span + c0 + STEP] = real
+
+    def own_tile(src, dst, i):
+        t = dot_t(left[:, :depth], src[0, rows(i), :]) + dot_t(left[:, depth:], src[1, rows(i), :])
+        t = t.astype(BF16)
+        dst[:, cols(i, 0)] = t[:span]
+        dst[:, cols(i, span)] = t[span:]
+
+    def their_tile(src, dst, i):
+        t = dot_t(src[0, rows(i), :], left[:, :depth]) + dot_t(src[1, rows(i), :], left[:, depth:])
+        dst[rows(i), :] = t.astype(BF16)
+
+    def put(t, k, j):
+        return pltpu.make_async_copy(res.at[t, k], out.at[t, k], out_sem.at[j])
+
+    def emit(t, k, src, j):
+        f = jnp.dot(src[...], weights[...], preferred_element_type=F32)
+        res[t, k, 0] = (rec_v[t, k, 0].astype(F32) - f[:, :span]).astype(BF16)
+        res[t, k, 1] = (rec_v[t, k, 1].astype(F32) - f[:, span:]).astype(BF16)
+        put(t, k, j).start()
+
+    def each(body):
+        def step(i, carry):
+            body(i)
+            return carry
+        lax.fori_loop(0, pieces, step, 0)
+
+    load.wait()
+
+    @each
+    def _(i):
+        mate_copy(i).wait_recv()
+        own_tile(buf_m, tile, i)
+
+    emit(0, core, tile, 0)
+
+    @each
+    def _(i):
+        @pl.when(owner)
+        def _():
+            row_copy(i).wait_recv()
+            share_c(i).start()
+
+        z_copy(i).wait_recv()
+        fwd_copy(i).start()
+
+        @pl.when(owner)
+        def _():
+            their_tile(buf_c, send_c, i)
+        their_tile(buf_a, send_a, i)
+
+        @pl.when(owner)
+        def _():
+            own_tile(buf_c, tile3, i)
+        own_tile(buf_a, tile, i)
+
+    tile_a.start()
+
+    @pl.when(owner)
+    def _():
+        tile_c.start()
+        emit(1, side, tile3, 3)
+    emit(2, side, tile, 1)
+
+    @pl.when(giver)
+    def _():
+        @each
+        def _(i):
+            share_c(i).wait_recv()
+            own_tile(buf_d, tile3, i)
+        emit(0, 1 - core, tile3, 4)
+
+    @each
+    def _(i):
+        fwd_copy(i).wait_recv()
+
+        @pl.when(giver)
+        def _():
+            share_b(i).start()
+        own_tile(buf_b, tile2, i)
+
+        @pl.when(owner)
+        def _():
+            share_b(i).wait_recv()
+            own_tile(buf_d, tile3, i)
+
+    emit(1, 1 - side, tile2, 2)
+
+    @pl.when(owner)
+    def _():
+        emit(0, 1 - core, tile3, 4)
+
+    tile_a.wait_recv()
+    emit(2, 1 - side, recv_a, 5)
+
+    @pl.when(giver)
+    def _():
+        tile_c.wait_recv()
+        emit(1, side, recv_c, 3)
+
+    for i in range(pieces):
+        z_copy(i).wait_send()
+        fwd_copy(i).wait_send()
+        mate_copy(i).wait_send()
+        share_c(i).wait_send()
+    tile_a.wait_send()
+
+    @pl.when(giver)
+    def _():
+        for i in range(pieces):
+            row_copy(i).wait_send()
+
+    @pl.when(owner)
+    def _():
+        tile_c.wait_send()
+
+    put(0, core, 0).wait()
+    put(2, side, 1).wait()
+    put(1, 1 - side, 2).wait()
+    put(1, side, 3).wait()
+    put(0, 1 - core, 4).wait()
+    put(2, 1 - side, 5).wait()
+
+
+def ladder(wavefield, recorded, match_filter):
+    n = lax.axis_size("shot")
+    _, span, depth = wavefield.shape
+    pieces = span // STEP
+    slots = recorded.shape[0]
+    block = pltpu.VMEM((2, span, depth), BF16)
+    flat = pltpu.VMEM((span, 2 * span), BF16)
+    return pl.pallas_call(
+        functools.partial(kernel, n),
+        out_shape=jax.ShapeDtypeStruct(recorded.shape, recorded.dtype),
+        in_specs=[
+            pl.BlockSpec(memory_space=pltpu.SMEM),
+            pl.BlockSpec(memory_space=pltpu.VMEM),
+            pl.BlockSpec(memory_space=pl.ANY),
+        ],
+        out_specs=pl.BlockSpec(memory_space=pl.ANY),
+        scratch_shapes=[
+            pltpu.VMEM((2 * span, 2 * depth), BF16),
+            pltpu.VMEM((2 * span, 2 * span), BF16),
+            block, block, block, block, block,
+            flat, flat, flat, flat, flat, flat, flat,
+            pltpu.VMEM(recorded.shape, BF16),
+            pltpu.VMEM(recorded.shape, BF16),
+            pltpu.SemaphoreType.DMA((5 * pieces + 2,)),
+            pltpu.SemaphoreType.DMA((5 * pieces + 2,)),
+            pltpu.SemaphoreType.DMA,
+            pltpu.SemaphoreType.DMA((2 * slots,)),
+        ],
+        compiler_params=pltpu.CompilerParams(
+            collective_id=0, has_side_effects=True, vmem_limit_bytes=56 * 2**20
+        ),
+    )(match_filter.astype(F32), wavefield, recorded)
 
 
 def passed_along(value, axis, steps):
@@ -38,6 +321,9 @@
 
 def shards(wavefield, recorded, match_filter):
     cycle_size = lax.axis_size("shot")
+    doubling = cycle_size // 8 == 2 and cycle_size // 4 == 4
+    if doubling and cycle_size % 4 == 0 and wavefield.shape[1] % STEP == 0:
+        return ladder(wavefield, recorded, match_filter)
     block_span_width = wavefield.shape[1]
     weights = filter_weights(match_filter, block_span_width)
     real_component = wavefield[0]

time: 122 us -> 76.3 us (0.63)
  Pallas kernels: 0 us -> 70.7 us
  waiting for transfers between devices: 46.1 us -> 0 us
  other arithmetic: 33.7 us -> 1.22 us
  local copies, waits for them, and re-layouts: 22.5 us -> 4.16 us
  matrix products: 10.1 us -> 0 us
  starting transfers between devices: 7.01 us -> 0 us
  loops' own time: 1.65 us -> 0 us
    pallas_call x0 -> x1, Pallas kernels: none -> 70.7 us  [ladder(): pl.pallas_call(functools.partial(kernel, n), out_shape=jax.ShapeDtypeStru...]
    ppermute x6 -> x0, waiting for transfers between devices: 46.1 us -> none  [passed_along(): return lax.ppermute(value, axis, pairs)]
    select_n x63 -> x0, other arithmetic: 24.5 us -> none  [place_tap(): jnp.where((lag_index == tap_index)[None], column[:, :, None], carried)]
    dot_general x9 -> x0, matrix products: 10.1 us -> none  [the longest x3 5.42 us: shards(): lax.dot_general(left_rows, right_rows, (((1,), (1,)), ((), ())), preferre...]
    eq x63 -> x0, other arithmetic: 8.06 us -> none  [place_tap(): lag_index == tap_index]
    ppermute x6 -> x0, starting transfers between devices: 7.01 us -> none  [passed_along(): return lax.ppermute(value, axis, pairs)]
    unnamed x19 -> x1, local copies, waits for them, and re-layouts: 9.93 us -> 4.16 us
    squeeze x4 -> x0, local copies, waits for them, and re-layouts: 4.59 us -> none  [the longest x3 4.47 us: shards(): right_rows = jnp.concatenate([ahead_data[0], ahead_data[1]], 1)]
  transfers between devices with their start and end apart: 6 -> 0, of which waited for: 3 -> 0; matrix products, arithmetic and copies ran while one was open for 48% -> 0% of each run, Pallas kernels for 0% -> 0%
where the time goes in v1:
time: 76.3 us; the launch traced here: 76.1 us
  Pallas kernels  70.7 us (93%)
  local copies, waits for them, and re-layouts  4.16 us (5%)
  other arithmetic  1.22 us (2%)
    pallas_call x1, Pallas kernels, ladder(): pl.pallas_call(functools.partial(kernel, n), out_shape=jax.ShapeDtypeStru...  70.7 us
    unnamed x1, local copies, waits for them, and re-layouts  4.16 us

profile of v1, /device:TPU:0, one launch (start us, length us, event | category | flops | bytes accessed | tf_op | source)
XLA Modules:
  0.0 76.1 jit_solution(18068124459616597886)
XLA Ops:
  0.0 1.2 %convert_element_type.3.mf = f32[2,63]{1,0:T(2,128)} convert(bf16[2,63]{1,0:T(2,128)(2,1)} %param.5) | non-fusion elementwise | flops 126 | bytes 756 | tf_op jit(solution)/shard_map/convert_element_type | solution.py:287
  1.2 70.7 %shard_map.37 = bf16[3,2,2,384,384]{4,3,2,1,0:T(8,128)(2,1)} custom-call(f32[2,63]{1,0:T(2,128)} %convert_element_type.3.mf, bf16[2,384,1024]{2,1,0:T(8,128)(2,1)} %wave.1, bf16[3,2,2,384,384]{4,3,2,1,0:T(8,128)(2,1)} %rec.1), custom_call_target="tpu_custom_call" | custom-call | tf_op jit(solution)/shard_map/pallas_call | solution.py:263
  72.0 4.2 %copy.5 = bf16[3,2,2,384,384]{4,3,2,1,0:T(8,128)(2,1)} copy(bf16[3,2,2,384,384]{4,3,2,1,0:T(8,128)(2,1)} %shard_map.37) | data formatting | bytes 7077888

commit v2 on v1

v2 whole, which is shorter than its diff:
```python
import functools

import jax
import jax.numpy as jnp
from jax import lax
from jax.experimental import pallas as pl
from jax.experimental.pallas import tpu as pltpu
from jax.sharding import PartitionSpec as P

MESH = pl.DeviceIdType.MESH
STEP = 128
CH_A, CH_B, CH_C, CH_M, CH_D, CH_TA, CH_TX = range(7)
LIMIT = 40 * 2**20
F32 = jnp.float32
BF16 = jnp.bfloat16


def dot_t(a, b):
    return lax.dot_general(a, b, (((1,), (1,)), ((), ())), preferred_element_type=F32)


def kernel(
    n, mf, wave, rec, out,
    wave_v, left, weights, buf_a, buf_b, buf_c, buf_m, buf_d,
    send_a, send_x, recv_a, recv_x, tile, tile2, tile3, rec_v, res, taps_row,
    ssem, rsem, in_sem, out_sem,
):
    span, depth = wave_v.shape[1], wave_v.shape[2]
    pieces = span // STEP
    half = (mf.shape[1] - 1) // 2
    me = lax.axis_index("shot")
    core = lax.rem(me, 2)
    side = lax.rem(me // 2, 2)
    mate = me + 1 - 2 * core
    across = me + 2 - 4 * side
    beyond = lax.rem(me + n - 2 + 4 * side, n)
    up, down = lax.rem(me + 4, n), lax.rem(me + n - 4, n)
    z_to = (1 - side) * down + side * up
    z_from = (1 - side) * up + side * down
    owner = (core == side)
    giver = (core != side)

    load_wave = pltpu.make_async_copy(wave, wave_v, in_sem.at[0])
    load_wave.start()
    load = pltpu.make_async_copy(rec, rec_v, in_sem.at[1])
    load.start()

    barrier = pltpu.get_barrier_semaphore()
    for other in (mate, across, beyond, up, down):
        pl.semaphore_signal(barrier, inc=1, device_id={"shot": other}, device_id_type=MESH)
    pl.semaphore_wait(barrier, 5)

    def remote(src, dst, sem, target):
        return pltpu.make_async_remote_copy(
            src_ref=src, dst_ref=dst, send_sem=ssem.at[sem], recv_sem=rsem.at[sem],
            device_id={"shot": target}, device_id_type=MESH,
        )

    def rows(i):
        if isinstance(i, int):
            return pl.ds(i * STEP, STEP)
        return pl.ds(pl.multiple_of(i * STEP, STEP), STEP)

    def cols(i, base):
        return pl.ds(pl.multiple_of(base + i * STEP, STEP), STEP)

    def piece(src, dst, channel, i, target):
        return remote(
            src.at[:, rows(i), :], dst.at[:, rows(i), :], channel * pieces + i, target
        )

    def tile_piece(src, dst, channel, i, target):
        return remote(src.at[rows(i), :], dst.at[rows(i), :], channel * pieces + i, target)

    def z_copy(i):
        return piece(wave, buf_a, CH_A, i, z_to)

    def fwd_copy(i):
        return piece(buf_a, buf_b, CH_B, i, across)

    def row_copy(i):
        return piece(wave, buf_c, CH_C, i, across)

    def mate_copy(i):
        return piece(wave, buf_m, CH_M, i, mate)

    def share_c(i):
        return piece(buf_c, buf_d, CH_D, i, mate)

    def share_b(i):
        return piece(buf_b, buf_d, CH_D, i, mate)

    def tile_a(i):
        return tile_piece(send_a, recv_a, CH_TA, i, z_from)

    def tile_b(i):
        return tile_piece(send_x, recv_x, CH_TX, i, beyond)

    def tile_c(i):
        return tile_piece(send_x, recv_x, CH_TX, i, across)

    @pl.when(giver)
    def _():
        for i in range(pieces):
            row_copy(i).start()

    for i in range(pieces):
        z_copy(i).start()
    for i in range(pieces):
        mate_copy(i).start()

    width = taps_row.shape[1]
    taps_row[...] = jnp.zeros_like(taps_row)
    taps_row[0:2, 0:mf.shape[1]] = mf[...].astype(F32)
    row_id = lax.broadcasted_iota(jnp.int32, (span, width), 0)
    banded = []
    for c in range(2):
        x = jnp.broadcast_to(taps_row[c:c + 1, :], (span, width))
        x = pltpu.roll(x, width - half, 1)
        bit = 1
        while bit < span:
            x = jnp.where((row_id // bit) % 2 == 1, pltpu.roll(x, bit, 1), x)
            bit *= 2
        banded.append(x[:, :span].astype(BF16))
    weights[:span, :span] = banded[0]
    weights[:span, span:] = -banded[1]
    weights[span:, :span] = banded[1]
    weights[span:, span:] = banded[0]

    load_wave.wait()
    left[:span, :depth] = wave_v[0]
    left[:span, depth:] = -wave_v[1]
    left[span:, :depth] = wave_v[1]
    left[span:, depth:] = wave_v[0]

    def own_tile(src, dst, i):
        t = dot_t(left[:, :depth], src[0, rows(i), :]) + dot_t(left[:, depth:], src[1, rows(i), :])
        t = t.astype(BF16)
        dst[:, cols(i, 0)] = t[:span]
        dst[:, cols(i, span)] = t[span:]

    def their_tile(src, dst, i):
        t = dot_t(src[0, rows(i), :], left[:, :depth]) + dot_t(src[1, rows(i), :], left[:, depth:])
        dst[rows(i), :] = t.astype(BF16)

    def put(t, k, i, j):
        return pltpu.make_async_copy(
            res.at[t, k, :, rows(i), :], out.at[t, k, :, rows(i), :], out_sem.at[j * pieces + i]
        )

    def emit(t, k, src, i, j):
        f = dot_t(src[rows(i), :], weights[...])
        res[t, k, 0, rows(i), :] = (rec_v[t, k, 0, rows(i), :].astype(F32) - f[:, :span]).astype(BF16)
        res[t, k, 1, rows(i), :] = (rec_v[t, k, 1, rows(i), :].astype(F32) - f[:, span:]).astype(BF16)
        put(t, k, i, j).start()

    def each(body):
        def step(i, carry):
            body(i)
            return carry
        lax.fori_loop(0, pieces, step, 0)

    load.wait()

    @each
    def _(i):
        mate_copy(i).wait_recv()
        own_tile(buf_m, tile, i)

    each(lambda i: emit(0, core, tile, i, 0))

    @pl.when(owner)
    def _():
        @each
        def _(i):
            row_copy(i).wait_recv()
            share_c(i).start()
            z_copy(i).wait_recv()
            fwd_copy(i).start()
            their_tile(buf_c, send_x, i)
            tile_c(i).start()
            their_tile(buf_a, send_a, i)
            tile_a(i).start()
            own_tile(buf_c, tile3, i)
            own_tile(buf_a, tile, i)

        @each
        def _(i):
            emit(1, side, tile3, i, 3)
            emit(2, side, tile, i, 1)

        @each
        def _(i):
            share_b(i).wait_recv()
            own_tile(buf_d, tile2, i)

        each(lambda i: emit(0, 1 - core, tile2, i, 4))

        @each
        def _(i):
            tile_a(i).wait_recv()
            emit(2, 1 - side, recv_a, i, 5)
            tile_b(i).wait_recv()
            emit(1, 1 - side, recv_x, i, 2)

        @each
        def _(i):
            share_c(i).wait_send()
            fwd_copy(i).wait_send()
            tile_c(i).wait_send()

    @pl.when(giver)
    def _():
        @each
        def _(i):
            z_copy(i).wait_recv()
            their_tile(buf_a, send_a, i)
            tile_a(i).start()
            own_tile(buf_a, tile, i)
            share_c(i).wait_recv()
            own_tile(buf_d, tile3, i)
            fwd_copy(i).wait_recv()
            share_b(i).start()
            their_tile(buf_b, send_x, i)
            tile_b(i).start()
            own_tile(buf_b, tile2, i)

        @each
        def _(i):
            emit(2, side, tile, i, 1)
            emit(0, 1 - core, tile3, i, 4)
            emit(1, 1 - side, tile2, i, 2)

        @each
        def _(i):
            tile_c(i).wait_recv()
            emit(1, side, recv_x, i, 3)

        @each
        def _(i):
            tile_a(i).wait_recv()
            emit(2, 1 - side, recv_a, i, 5)

        @each
        def _(i):
            row_copy(i).wait_send()
            share_b(i).wait_send()
            tile_b(i).wait_send()

    @each
    def _(i):
        z_copy(i).wait_send()
        mate_copy(i).wait_send()
        tile_a(i).wait_send()
        put(0, core, i, 0).wait()
        put(2, side, i, 1).wait()
        put(1, 1 - side, i, 2).wait()
        put(1, side, i, 3).wait()
        put(0, 1 - core, i, 4).wait()
        put(2, 1 - side, i, 5).wait()


def ladder(wavefield, recorded, match_filter):
    n = lax.axis_size("shot")
    _, span, depth = wavefield.shape
    pieces = span // STEP
    slots = recorded.shape[0]
    width = -(-(span + match_filter.shape[1]) // STEP) * STEP
    block = pltpu.VMEM((2, span, depth), BF16)
    flat = pltpu.VMEM((span, 2 * span), BF16)
    return pl.pallas_call(
        functools.partial(kernel, n),
        out_shape=jax.ShapeDtypeStruct(recorded.shape, recorded.dtype),
        in_specs=[
            pl.BlockSpec(memory_space=pltpu.VMEM),
            pl.BlockSpec(memory_space=pltpu.HBM),
            pl.BlockSpec(memory_space=pltpu.HBM),
        ],
        out_specs=pl.BlockSpec(memory_space=pl.ANY),
        scratch_shapes=[
            block,
            pltpu.VMEM((2 * span, 2 * depth), BF16),
            pltpu.VMEM((2 * span, 2 * span), BF16),
            block, block, block, block, block,
            flat, flat, flat, flat, flat, flat, flat,
            pltpu.VMEM(recorded.shape, BF16),
            pltpu.VMEM(recorded.shape, BF16),
            pltpu.VMEM((8, width), F32),
            pltpu.SemaphoreType.DMA((7 * pieces,)),
            pltpu.SemaphoreType.DMA((7 * pieces,)),
            pltpu.SemaphoreType.DMA((2,)),
            pltpu.SemaphoreType.DMA((2 * slots * pieces,)),
        ],
        compiler_params=pltpu.CompilerParams(
            collective_id=0, has_side_effects=True, vmem_limit_bytes=LIMIT
        ),
    )(match_filter, wavefield, recorded)


def passed_along(value, axis, steps):
    count = lax.axis_size(axis)
    pairs = [(source, (source + steps) % count) for source in range(count)]
    return lax.ppermute(value, axis, pairs)


def toeplitz(match_filter, block_span_width):
    tap_count = match_filter.shape[1]
    half_taps = (tap_count - 1) // 2
    row_index = lax.broadcasted_iota(jnp.int32, (block_span_width, block_span_width), 0)
    col_index = lax.broadcasted_iota(jnp.int32, (block_span_width, block_span_width), 1)
    lag_index = row_index - col_index + half_taps
    coeffs = match_filter.astype(jnp.float32)

    def place_tap(tap_index, carried):
        column = lax.dynamic_slice_in_dim(coeffs, tap_index, 1, 1)
        return jnp.where((lag_index == tap_index)[None], column[:, :, None], carried)

    return lax.fori_loop(
        0, tap_count, place_tap, jnp.zeros((2, block_span_width, block_span_width), jnp.float32)
    )


def filter_weights(match_filter, block_span_width):
    toe_pair = toeplitz(match_filter, block_span_width)
    real_component = toe_pair[0].astype(jnp.bfloat16)
    imag_part = toe_pair[1].astype(jnp.bfloat16)
    return jnp.stack(
        [jnp.stack([real_component, imag_part], 1), jnp.stack([-imag_part, real_component], 1)], 0
    )


def shards(wavefield, recorded, match_filter):
    cycle_size = lax.axis_size("shot")
    doubling = cycle_size // 8 == 2 and cycle_size // 4 == 4
    if doubling and cycle_size % 4 == 0 and wavefield.shape[1] % STEP == 0:
        return ladder(wavefield, recorded, match_filter)
    block_span_width = wavefield.shape[1]
    weights = filter_weights(match_filter, block_span_width)
    real_component = wavefield[0]
    imag_part = wavefield[1]
    left_rows = jnp.concatenate(
        [
            jnp.concatenate([real_component, -imag_part], 1),
            jnp.concatenate([imag_part, real_component], 1),
        ],
        0,
    )
    results = []
    for slot_index, offset in enumerate((1, cycle_size // 8, cycle_size // 4)):
        ahead_data = passed_along(wavefield, "shot", -offset)
        right_rows = jnp.concatenate([ahead_data[0], ahead_data[1]], 1)
        stacked = lax.dot_general(
            left_rows, right_rows, (((1,), (1,)), ((), ())), preferred_element_type=jnp.float32
        )
        forward_tile = stacked.astype(jnp.bfloat16).reshape(2, block_span_width, block_span_width)
        ahead_filtered = jnp.einsum(
            "csq,cqdx->dsx", forward_tile, weights, preferred_element_type=jnp.float32
        )
        received = passed_along(forward_tile, "shot", offset)
        behind_filtered = jnp.einsum(
            "csr,csdx->drx", received, weights, preferred_element_type=jnp.float32
        )
        ahead_out = (recorded[slot_index, 0].astype(jnp.float32) - ahead_filtered).astype(
            jnp.bfloat16
        )
        behind_out = (recorded[slot_index, 1].astype(jnp.float32) - behind_filtered).astype(
            jnp.bfloat16
        )
        results.append(jnp.stack([ahead_out, behind_out]))
    return jnp.stack(results)


def solution(mesh):
    return jax.shard_map(
        shards,
        mesh=mesh,
        in_specs=(P("freq", "shot", None), P("freq", None, None, "shot", None), P()),
        out_specs=P("freq", None, None, "shot", None),
        check_vma=False,
    )
```

time: 76.3 us -> 71.4 us (0.936)
  the two profiles are of different devices: /device:TPU:0 before, /device:TPU:10 now
where the time goes in v2:
time: 71.4 us; the launch traced here: 71.2 us
  Pallas kernels  65.4 us (92%)
  local copies, waits for them, and re-layouts  5.86 us (8%)
    pallas_call x1, Pallas kernels, ladder(): pl.pallas_call(functools.partial(kernel, n), out_shape=jax.ShapeDtypeStru...  65.4 us
    unnamed x7, local copies, waits for them, and re-layouts  5.86 us

profile of v2, /device:TPU:10, one launch (start us, length us, event | category | flops | bytes accessed | tf_op | source)
XLA Modules:
  0.0 71.2 jit_solution(5361321464745076444)
XLA Ops:
  0.0 0.0 copy-start
  0.0 2.0 %copy-done = bf16[3,2,2,384,384]{4,3,2,1,0:T(8,128)(2,1)S(1)} copy-done((bf16[3,2,2,384,384]{4,3,2,1,0:T(8,128)(2,1)S(1)}, bf16[3,2,2,384,384]{4,3,2,1,0:T(8,128)(2,1)}, u32[]{:S(2)}) %copy-start) | copy-done | bytes 3538968
  2.0 0.0 copy-start.1
  2.0 1.4 %copy-done.1 = bf16[2,384,1024]{2,1,0:T(8,128)(2,1)S(1)} copy-done((bf16[2,384,1024]{2,1,0:T(8,128)(2,1)S(1)}, bf16[2,384,1024]{2,1,0:T(8,128)(2,1)}, u32[]{:S(2)}) %copy-start.1) | copy-done | bytes 1572888
  3.4 0.0 copy-start.2
  3.4 0.7 copy-done.2
  4.1 65.4 %shard_map.37 = bf16[3,2,2,384,384]{4,3,2,1,0:T(8,128)(2,1)S(1)} custom-call(bf16[2,63]{1,0:T(2,128)(2,1)S(1)} %copy-done.2, bf16[2,384,1024]{2,1,0:T(8,128)(2,1)S(1)} %copy-done.1, bf16[3,2,2,384,384]{4,3,2,1,0:T(8,128)(2,1)S(1)} %copy-done), custom_call_target="tpu_custom_call" | custom-call | tf_op jit(solution)/shard_map/pallas_call | solution.py:271
  69.4 1.8 %copy.5 = bf16[3,2,2,384,384]{4,3,2,1,0:T(8,128)(2,1)} copy(bf16[3,2,2,384,384]{4,3,2,1,0:T(8,128)(2,1)S(1)} %shard_map.37) | data formatting | bytes 7077888
Async XLA Ops:
  0.0 2.0 %copy-start = (bf16[3,2,2,384,384]{4,3,2,1,0:T(8,128)(2,1)S(1)}, bf16[3,2,2,384,384]{4,3,2,1,0:T(8,128)(2,1)}, u32[]{:S(2)}) copy-start(bf16[3,2,2,384,384]{4,3,2,1,0:T(8,128)(2,1)} %rec.1) | copy-start | bytes 10616836
  2.0 1.4 %copy-start.1 = (bf16[2,384,1024]{2,1,0:T(8,128)(2,1)S(1)}, bf16[2,384,1024]{2,1,0:T(8,128)(2,1)}, u32[]{:S(2)}) copy-start(bf16[2,384,1024]{2,1,0:T(8,128)(2,1)} %wave.1) | copy-start | bytes 4718596
  3.4 0.7 copy-start.2

commit v3 on v2

--- a/solution.py
+++ b/solution.py
@@ -20,8 +20,8 @@
 
 
 def kernel(
-    n, mf, wave, rec, out,
-    wave_v, left, weights, buf_a, buf_b, buf_c, buf_m, buf_d,
+    n, mf_hbm, wave, rec, out,
+    mf, wave_v, left, weights, buf_a, buf_b, buf_c, buf_m, buf_d,
     send_a, send_x, recv_a, recv_x, tile, tile2, tile3, rec_v, res, taps_row,
     ssem, rsem, in_sem, out_sem,
 ):
@@ -40,6 +40,8 @@
     owner = (core == side)
     giver = (core != side)
 
+    load_taps = pltpu.make_async_copy(mf_hbm, mf, in_sem.at[2])
+    load_taps.start()
     load_wave = pltpu.make_async_copy(wave, wave_v, in_sem.at[0])
     load_wave.start()
     load = pltpu.make_async_copy(rec, rec_v, in_sem.at[1])
@@ -109,6 +111,7 @@
     for i in range(pieces):
         mate_copy(i).start()
 
+    load_taps.wait()
     width = taps_row.shape[1]
     taps_row[...] = jnp.zeros_like(taps_row)
     taps_row[0:2, 0:mf.shape[1]] = mf[...].astype(F32)
@@ -272,12 +275,13 @@
         functools.partial(kernel, n),
         out_shape=jax.ShapeDtypeStruct(recorded.shape, recorded.dtype),
         in_specs=[
-            pl.BlockSpec(memory_space=pltpu.VMEM),
+            pl.BlockSpec(memory_space=pltpu.HBM),
             pl.BlockSpec(memory_space=pltpu.HBM),
             pl.BlockSpec(memory_space=pltpu.HBM),
         ],
         out_specs=pl.BlockSpec(memory_space=pl.ANY),
         scratch_shapes=[
+            pltpu.VMEM(match_filter.shape, BF16),
             block,
             pltpu.VMEM((2 * span, 2 * depth), BF16),
             pltpu.VMEM((2 * span, 2 * span), BF16),
@@ -288,13 +292,13 @@
             pltpu.VMEM((8, width), F32),
             pltpu.SemaphoreType.DMA((7 * pieces,)),
             pltpu.SemaphoreType.DMA((7 * pieces,)),
-            pltpu.SemaphoreType.DMA((2,)),
+            pltpu.SemaphoreType.DMA((3,)),
             pltpu.SemaphoreType.DMA((2 * slots * pieces,)),
         ],
         compiler_params=pltpu.CompilerParams(
             collective_id=0, has_side_effects=True, vmem_limit_bytes=LIMIT
         ),
-    )(match_filter, wavefield, recorded)
+    )(*(pltpu.with_memory_space_constraint(x, pltpu.HBM) for x in (match_filter, wavefield, recorded)))
 
 
 def passed_along(value, axis, steps):

time: 71.4 us -> 67 us (0.938)
  local copies, waits for them, and re-layouts: 5.86 us -> 1.8 us
    unnamed x7 -> x1, local copies, waits for them, and re-layouts: 5.86 us -> 1.8 us
where the time goes in v3:
time: 67 us; the launch traced here: 66.8 us
  Pallas kernels  65 us (97%)
  local copies, waits for them, and re-layouts  1.8 us (3%)
    pallas_call x1, Pallas kernels, ladder(): pl.pallas_call(functools.partial(kernel, n), out_shape=jax.ShapeDtypeStru...  65 us
    unnamed x1, local copies, waits for them, and re-layouts  1.8 us

profile of v3, /device:TPU:10, one launch (start us, length us, event | category | flops | bytes accessed | tf_op | source)
XLA Modules:
  0.0 66.8 jit_solution(7657442052130499975)
XLA Ops:
  0.0 65.0 %shard_map.37 = bf16[3,2,2,384,384]{4,3,2,1,0:T(8,128)(2,1)S(1)} custom-call(bf16[2,63]{1,0:T(2,128)(2,1)} %mf_hbm.1, bf16[2,384,1024]{2,1,0:T(8,128)(2,1)} %wave.1, bf16[3,2,2,384,384]{4,3,2,1,0:T(8,128)(2,1)} %rec.1), custom_call_target="tpu_custom_call" | custom-call | tf_op jit(solution)/shard_map/pallas_call | solution.py:274
  65.0 1.8 %copy.5 = bf16[3,2,2,384,384]{4,3,2,1,0:T(8,128)(2,1)} copy(bf16[3,2,2,384,384]{4,3,2,1,0:T(8,128)(2,1)S(1)} %shard_map.37) | data formatting | bytes 7077888

commit v4 on v3

--- a/solution.py
+++ b/solution.py
@@ -23,7 +23,7 @@
     n, mf_hbm, wave, rec, out,
     mf, wave_v, left, weights, buf_a, buf_b, buf_c, buf_m, buf_d,
     send_a, send_x, recv_a, recv_x, tile, tile2, tile3, rec_v, res, taps_row,
-    ssem, rsem, in_sem, out_sem,
+    ssem, rsem, in_sem, out_sem, go_sem,
 ):
     span, depth = wave_v.shape[1], wave_v.shape[2]
     pieces = span // STEP
@@ -95,19 +95,26 @@
     def tile_a(i):
         return tile_piece(send_a, recv_a, CH_TA, i, z_from)
 
+    tail = pl.ds(STEP, span - STEP)
+
     def tile_b(i):
-        return tile_piece(send_x, recv_x, CH_TX, i, beyond)
+        return remote(
+            send_x.at[:, rows(i), tail], recv_x.at[:, rows(i), tail], CH_TX * pieces + i, beyond
+        )
 
     def tile_c(i):
-        return tile_piece(send_x, recv_x, CH_TX, i, across)
+        return piece(send_x, recv_x, CH_TX, i, across)
 
     @pl.when(giver)
     def _():
         for i in range(pieces):
             row_copy(i).start()
 
-    for i in range(pieces):
-        z_copy(i).start()
+    @pl.when(owner)
+    def _():
+        for i in range(pieces):
+            z_copy(i).start()
+
     for i in range(pieces):
         mate_copy(i).start()
 
@@ -146,13 +153,25 @@
         t = dot_t(src[0, rows(i), :], left[:, :depth]) + dot_t(src[1, rows(i), :], left[:, depth:])
         dst[rows(i), :] = t.astype(BF16)
 
+    def their_pair(src, dst, i):
+        t = dot_t(src[0, rows(i), :], left[:, :depth]) + dot_t(src[1, rows(i), :], left[:, depth:])
+        t = t.astype(BF16)
+        dst[0, rows(i), :] = t[:, :span]
+        dst[1, rows(i), :] = t[:, span:]
+
     def put(t, k, i, j):
         return pltpu.make_async_copy(
             res.at[t, k, :, rows(i), :], out.at[t, k, :, rows(i), :], out_sem.at[j * pieces + i]
         )
 
     def emit(t, k, src, i, j):
-        f = dot_t(src[rows(i), :], weights[...])
+        store(t, k, dot_t(src[rows(i), :], weights[...]), i, j)
+
+    def emit_pair(t, k, src, i, j):
+        f = dot_t(src[0, rows(i), :], weights[:, :span])
+        store(t, k, f + dot_t(src[1, rows(i), :], weights[:, span:]), i, j)
+
+    def store(t, k, f, i, j):
         res[t, k, 0, rows(i), :] = (rec_v[t, k, 0, rows(i), :].astype(F32) - f[:, :span]).astype(BF16)
         res[t, k, 1, rows(i), :] = (rec_v[t, k, 1, rows(i), :].astype(F32) - f[:, span:]).astype(BF16)
         put(t, k, i, j).start()
@@ -176,14 +195,19 @@
     def _():
         @each
         def _(i):
+            z_copy(i).wait_recv()
+            fwd_copy(i).start()
+
+            @pl.when(i == pieces // 2)
+            def _():
+                pl.semaphore_signal(go_sem, inc=1, device_id={"shot": mate}, device_id_type=MESH)
+
+            their_tile(buf_a, send_a, i)
+            tile_a(i).start()
             row_copy(i).wait_recv()
             share_c(i).start()
-            z_copy(i).wait_recv()
-            fwd_copy(i).start()
-            their_tile(buf_c, send_x, i)
+            their_pair(buf_c, send_x, i)
             tile_c(i).start()
-            their_tile(buf_a, send_a, i)
-            tile_a(i).start()
             own_tile(buf_c, tile3, i)
             own_tile(buf_a, tile, i)
 
@@ -191,6 +215,12 @@
         def _(i):
             emit(1, side, tile3, i, 3)
             emit(2, side, tile, i, 1)
+
+        fwd_copy(0).wait_recv()
+        t = dot_t(left[:, :depth], buf_b[0, :STEP, :]) + dot_t(left[:, depth:], buf_b[1, :STEP, :])
+        t = t.astype(BF16)
+        recv_x[0, :, :STEP] = t[:span]
+        recv_x[1, :, :STEP] = t[span:]
 
         @each
         def _(i):
@@ -204,7 +234,7 @@
             tile_a(i).wait_recv()
             emit(2, 1 - side, recv_a, i, 5)
             tile_b(i).wait_recv()
-            emit(1, 1 - side, recv_x, i, 2)
+            emit_pair(1, 1 - side, recv_x, i, 2)
 
         @each
         def _(i):
@@ -214,19 +244,28 @@
 
     @pl.when(giver)
     def _():
-        @each
-        def _(i):
+        pl.semaphore_wait(go_sem, 1)
+        for i in range(pieces):
+            z_copy(i).start()
+
+        @each
+        def _(i):
+            fwd_copy(i).wait_recv()
+            share_b(i).start()
+            their_pair(buf_b, send_x, i)
+            tile_b(i).start()
             z_copy(i).wait_recv()
+
+            @pl.when(i == 0)
+            def _():
+                fwd_copy(0).start()
+
             their_tile(buf_a, send_a, i)
             tile_a(i).start()
             own_tile(buf_a, tile, i)
+            own_tile(buf_b, tile2, i)
             share_c(i).wait_recv()
             own_tile(buf_d, tile3, i)
-            fwd_copy(i).wait_recv()
-            share_b(i).start()
-            their_tile(buf_b, send_x, i)
-            tile_b(i).start()
-            own_tile(buf_b, tile2, i)
 
         @each
         def _(i):
@@ -237,12 +276,14 @@
         @each
         def _(i):
             tile_c(i).wait_recv()
-            emit(1, side, recv_x, i, 3)
+            emit_pair(1, side, recv_x, i, 3)
 
         @each
         def _(i):
             tile_a(i).wait_recv()
             emit(2, 1 - side, recv_a, i, 5)
+
+        fwd_copy(0).wait_send()
 
         @each
         def _(i):
@@ -271,6 +312,7 @@
     width = -(-(span + match_filter.shape[1]) // STEP) * STEP
     block = pltpu.VMEM((2, span, depth), BF16)
     flat = pltpu.VMEM((span, 2 * span), BF16)
+    pair = pltpu.VMEM((2, span, span), BF16)
     return pl.pallas_call(
         functools.partial(kernel, n),
         out_shape=jax.ShapeDtypeStruct(recorded.shape, recorded.dtype),
@@ -286,7 +328,7 @@
             pltpu.VMEM((2 * span, 2 * depth), BF16),
             pltpu.VMEM((2 * span, 2 * span), BF16),
             block, block, block, block, block,
-            flat, flat, flat, flat, flat, flat, flat,
+            flat, pair, flat, pair, flat, flat, flat,
             pltpu.VMEM(recorded.shape, BF16),
             pltpu.VMEM(recorded.shape, BF16),
             pltpu.VMEM((8, width), F32),
@@ -294,6 +336,7 @@
             pltpu.SemaphoreType.DMA((7 * pieces,)),
             pltpu.SemaphoreType.DMA((3,)),
             pltpu.SemaphoreType.DMA((2 * slots * pieces,)),
+            pltpu.SemaphoreType.REGULAR,
         ],
         compiler_params=pltpu.CompilerParams(
             collective_id=0, has_side_effects=True, vmem_limit_bytes=LIMIT
@@ -336,7 +379,7 @@
 def shards(wavefield, recorded, match_filter):
     cycle_size = lax.axis_size("shot")
     doubling = cycle_size // 8 == 2 and cycle_size // 4 == 4
-    if doubling and cycle_size % 4 == 0 and wavefield.shape[1] % STEP == 0:
+    if doubling and cycle_size % 4 == 0 and wavefield.shape[1] % STEP == 0 and wavefield.shape[1] > STEP:
         return ladder(wavefield, recorded, match_filter)
     block_span_width = wavefield.shape[1]
     weights = filter_weights(match_filter, block_span_width)

time: 67 us -> 73.8 us (1.10)
  the two profiles are of different devices: /device:TPU:10 before, /device:TPU:1 now
where the time goes in v4:
time: 73.8 us; the launch traced here: 73.7 us
  Pallas kernels  71.9 us (97%)
  local copies, waits for them, and re-layouts  1.8 us (2%)
    pallas_call x1, Pallas kernels, ladder(): pl.pallas_call(functools.partial(kernel, n), out_shape=jax.ShapeDtypeStru...  71.9 us
    unnamed x1, local copies, waits for them, and re-layouts  1.8 us

profile of v4, /device:TPU:1, one launch (start us, length us, event | category | flops | bytes accessed | tf_op | source)
XLA Modules:
  0.0 73.7 jit_solution(6423609126121220888)
XLA Ops:
  0.0 71.9 %shard_map.37 = bf16[3,2,2,384,384]{4,3,2,1,0:T(8,128)(2,1)S(1)} custom-call(bf16[2,63]{1,0:T(2,128)(2,1)} %mf_hbm.1, bf16[2,384,1024]{2,1,0:T(8,128)(2,1)} %wave.1, bf16[3,2,2,384,384]{4,3,2,1,0:T(8,128)(2,1)} %rec.1), custom_call_target="tpu_custom_call" | custom-call | tf_op jit(solution)/shard_map/pallas_call | solution.py:316
  71.9 1.8 %copy.5 = bf16[3,2,2,384,384]{4,3,2,1,0:T(8,128)(2,1)} copy(bf16[3,2,2,384,384]{4,3,2,1,0:T(8,128)(2,1)S(1)} %shard_map.37) | data formatting | bytes 7077888

commit v5 on v4

--- a/solution.py
+++ b/solution.py
@@ -23,7 +23,7 @@
     n, mf_hbm, wave, rec, out,
     mf, wave_v, left, weights, buf_a, buf_b, buf_c, buf_m, buf_d,
     send_a, send_x, recv_a, recv_x, tile, tile2, tile3, rec_v, res, taps_row,
-    ssem, rsem, in_sem, out_sem, go_sem,
+    ssem, rsem, in_sem, out_sem,
 ):
     span, depth = wave_v.shape[1], wave_v.shape[2]
     pieces = span // STEP
@@ -110,11 +110,8 @@
         for i in range(pieces):
             row_copy(i).start()
 
-    @pl.when(owner)
-    def _():
-        for i in range(pieces):
-            z_copy(i).start()
-
+    for i in range(pieces):
+        z_copy(i).start()
     for i in range(pieces):
         mate_copy(i).start()
 
@@ -198,10 +195,6 @@
             z_copy(i).wait_recv()
             fwd_copy(i).start()
 
-            @pl.when(i == pieces // 2)
-            def _():
-                pl.semaphore_signal(go_sem, inc=1, device_id={"shot": mate}, device_id_type=MESH)
-
             their_tile(buf_a, send_a, i)
             tile_a(i).start()
             row_copy(i).wait_recv()
@@ -244,28 +237,35 @@
 
     @pl.when(giver)
     def _():
-        pl.semaphore_wait(go_sem, 1)
-        for i in range(pieces):
-            z_copy(i).start()
-
-        @each
-        def _(i):
-            fwd_copy(i).wait_recv()
-            share_b(i).start()
-            their_pair(buf_b, send_x, i)
-            tile_b(i).start()
-            z_copy(i).wait_recv()
-
-            @pl.when(i == 0)
+        def step(i, carry):
+            @pl.when(i < pieces)
             def _():
-                fwd_copy(0).start()
-
-            their_tile(buf_a, send_a, i)
-            tile_a(i).start()
-            own_tile(buf_a, tile, i)
-            own_tile(buf_b, tile2, i)
-            share_c(i).wait_recv()
-            own_tile(buf_d, tile3, i)
+                z_copy(i).wait_recv()
+
+                @pl.when(i == 0)
+                def _():
+                    fwd_copy(0).start()
+
+                their_tile(buf_a, send_a, i)
+                tile_a(i).start()
+
+            @pl.when(i > 0)
+            def _():
+                fwd_copy(i - 1).wait_recv()
+                share_b(i - 1).start()
+                their_pair(buf_b, send_x, i - 1)
+                tile_b(i - 1).start()
+                own_tile(buf_b, tile2, i - 1)
+
+            @pl.when(i < pieces)
+            def _():
+                own_tile(buf_a, tile, i)
+                share_c(i).wait_recv()
+                own_tile(buf_d, tile3, i)
+
+            return carry
+
+        lax.fori_loop(0, pieces + 1, step, 0)
 
         @each
         def _(i):
@@ -336,7 +336,6 @@
             pltpu.SemaphoreType.DMA((7 * pieces,)),
             pltpu.SemaphoreType.DMA((3,)),
             pltpu.SemaphoreType.DMA((2 * slots * pieces,)),
-            pltpu.SemaphoreType.REGULAR,
         ],
         compiler_params=pltpu.CompilerParams(
             collective_id=0, has_side_effects=True, vmem_limit_bytes=LIMIT

time: 73.8 us -> 69.8 us (0.946)
  the two profiles are of different devices: /device:TPU:1 before, /device:TPU:10 now
where the time goes in v5:
time: 69.8 us; the launch traced here: 69.7 us
  Pallas kernels  67.9 us (97%)
  local copies, waits for them, and re-layouts  1.8 us (3%)
    pallas_call x1, Pallas kernels, ladder(): pl.pallas_call(functools.partial(kernel, n), out_shape=jax.ShapeDtypeStru...  67.9 us
    unnamed x1, local copies, waits for them, and re-layouts  1.8 us

profile of v5, /device:TPU:10, one launch (start us, length us, event | category | flops | bytes accessed | tf_op | source)
XLA Modules:
  0.0 69.7 jit_solution(2452453683589430476)
XLA Ops:
  0.0 67.9 %shard_map.37 = bf16[3,2,2,384,384]{4,3,2,1,0:T(8,128)(2,1)S(1)} custom-call(bf16[2,63]{1,0:T(2,128)(2,1)} %mf_hbm.1, bf16[2,384,1024]{2,1,0:T(8,128)(2,1)} %wave.1, bf16[3,2,2,384,384]{4,3,2,1,0:T(8,128)(2,1)} %rec.1), custom_call_target="tpu_custom_call" | custom-call | tf_op jit(solution)/shard_map/pallas_call | solution.py:316
  67.9 1.8 %copy.5 = bf16[3,2,2,384,384]{4,3,2,1,0:T(8,128)(2,1)} copy(bf16[3,2,2,384,384]{4,3,2,1,0:T(8,128)(2,1)S(1)} %shard_map.37) | data formatting | bytes 7077888

commit v6 on v3

--- a/solution.py
+++ b/solution.py
@@ -183,7 +183,12 @@
             their_tile(buf_c, send_x, i)
             tile_c(i).start()
             their_tile(buf_a, send_a, i)
-            tile_a(i).start()
+
+            @pl.when(i == pieces - 1)
+            def _():
+                for j in range(pieces):
+                    tile_a(j).start()
+
             own_tile(buf_c, tile3, i)
             own_tile(buf_a, tile, i)
 
@@ -218,7 +223,12 @@
         def _(i):
             z_copy(i).wait_recv()
             their_tile(buf_a, send_a, i)
-            tile_a(i).start()
+
+            @pl.when(i == pieces - 1)
+            def _():
+                for j in range(pieces):
+                    tile_a(j).start()
+
             own_tile(buf_a, tile, i)
             share_c(i).wait_recv()
             own_tile(buf_d, tile3, i)

time: 67 us -> 66.8 us (level)
  the two profiles are of different devices: /device:TPU:10 before, /device:TPU:1 now
where the time goes in v6:
time: 66.8 us; the launch traced here: 66.6 us
  Pallas kernels  64.8 us (97%)
  local copies, waits for them, and re-layouts  1.8 us (3%)
    pallas_call x1, Pallas kernels, ladder(): pl.pallas_call(functools.partial(kernel, n), out_shape=jax.ShapeDtypeStru...  64.8 us
    unnamed x1, local copies, waits for them, and re-layouts  1.8 us

profile of v6, /device:TPU:1, one launch (start us, length us, event | category | flops | bytes accessed | tf_op | source)
XLA Modules:
  0.0 66.6 jit_solution(10544176696651857831)
XLA Ops:
  0.0 64.8 %shard_map.37 = bf16[3,2,2,384,384]{4,3,2,1,0:T(8,128)(2,1)S(1)} custom-call(bf16[2,63]{1,0:T(2,128)(2,1)} %mf_hbm.1, bf16[2,384,1024]{2,1,0:T(8,128)(2,1)} %wave.1, bf16[3,2,2,384,384]{4,3,2,1,0:T(8,128)(2,1)} %rec.1), custom_call_target="tpu_custom_call" | custom-call | tf_op jit(solution)/shard_map/pallas_call | solution.py:284
  64.8 1.8 %copy.5 = bf16[3,2,2,384,384]{4,3,2,1,0:T(8,128)(2,1)} copy(bf16[3,2,2,384,384]{4,3,2,1,0:T(8,128)(2,1)S(1)} %shard_map.37) | data formatting | bytes 7077888
